TPU v7x, 128 devices: a whole 4x4x4 slice. The times are simulated.
128 devices in a mesh: space: 16 (over y_hi, x, core), code: 4 (over z), clip: 2 (over y_lo).
Axes of the slice: x: 4, y: 4 (y_hi: 2, y_lo: 2; y = y_hi * 2 + y_lo), z: 4, core: 2. Of those that a mesh axis runs over, the one named last changes fastest.
Arguments:
- soft_weights: bfloat16 [2, 1024, 32, 8192], P('clip', 'space', None, 'code'), may hold values from 0.00029945374 to 0.029907227
- codebook: bfloat16 [8192, 256], P('code'), may hold values from -6 to 6
- kernel_one: bfloat16 [3, 3, 256, 512], replicated, may hold values from -0.125 to 0.125
- kernel_two: bfloat16 [3, 3, 512, 512], replicated, may hold values from -0.09375 to 0.09375
- cotangent: bfloat16 [2, 1024, 32, 512], P('clip', ('space', 'code')), may hold values from -16 to 16
Outputs:
- decoded: bfloat16 [2, 1024, 32, 512], P('clip', ('space', 'code'))
- grad_one: float32 [3, 3, 256, 512], P(None, None, None, ('space', 'code', 'clip'))
- grad_two: float32 [3, 3, 512, 512], P(None, None, None, ('space', 'code', 'clip'))
- grad_codebook: float32 [8192, 256], P('code')
All inputs are finite; a program needn't handle non-finite values.
Results may differ from a plain program's by a relative error of at most 0.02.
Values may be sent and summed in bfloat16 or wider, within the bound.
A program may use at most 192 MiB of HBM per device.

v0:
```python
import jax
import jax.numpy as jnp
from jax import lax
from jax.sharding import PartitionSpec as P


def with_halo(block, sides, width):
    for axis, dim in sides:
        count = lax.axis_size(axis)
        forward = [(i, i + 1) for i in range(count - 1)]
        backward = [(target, source) for source, target in forward]
        low = lax.ppermute(
            lax.slice_in_dim(block, block.shape[dim] - width, None, axis=dim), axis, forward
        )
        high = lax.ppermute(lax.slice_in_dim(block, 0, width, axis=dim), axis, backward)
        block = jnp.concatenate([low, block, high], axis=dim)
    return block


def extend(field):
    grown = with_halo(field, ((("space", "code"), 0),), 1)
    return jnp.pad(grown, ((0, 0), (1, 1), (0, 0)))


def taps_forward(padded, kernel):
    height = padded.shape[0] - 2
    breadth = padded.shape[1] - 2
    accum = jnp.zeros((height * breadth, kernel.shape[3]), jnp.float32)
    for first in range(3):
        for second in range(3):
            window = padded[first : first + height, second : second + breadth].reshape(
                height * breadth, -1
            )
            accum = accum + jnp.dot(
                window, kernel[first, second], preferred_element_type=jnp.float32
            )
    return accum.reshape(height, breadth, -1)


def taps_back(padded, kernel):
    height = padded.shape[0] - 2
    breadth = padded.shape[1] - 2
    accum = jnp.zeros((height * breadth, kernel.shape[2]), jnp.float32)
    for first in range(3):
        for second in range(3):
            window = padded[
                2 - first : 2 - first + height, 2 - second : 2 - second + breadth
            ].reshape(height * breadth, -1)
            accum = accum + jnp.dot(
                window, kernel[first, second].T, preferred_element_type=jnp.float32
            )
    return accum.reshape(height, breadth, -1)


def kernel_grad(padded, upstream):
    height = upstream.shape[0]
    breadth = upstream.shape[1]
    flat_up = upstream.reshape(height * breadth, -1)
    result = []
    for first in range(3):
        line = []
        for second in range(3):
            window = padded[first : first + height, second : second + breadth].reshape(
                height * breadth, -1
            )
            line.append(
                lax.dot_general(
                    window, flat_up, (((0,), (0,)), ((), ())), preferred_element_type=jnp.float32
                )
            )
        result.append(jnp.stack(line))
    return jnp.stack(result)


def on_device(soft_weights, codebook, kernel_one, kernel_two, cotangent):
    weights = soft_weights[0]
    upstream = cotangent[0]
    own_rows = upstream.shape[0]
    breadth = weights.shape[1]
    code_slice = weights.shape[2]
    partial_value = jnp.dot(
        weights.reshape(-1, code_slice), codebook, preferred_element_type=jnp.float32
    )
    partial_value = partial_value.reshape(weights.shape[0], breadth, -1)
    summed = lax.psum(partial_value, "code")
    owned = lax.dynamic_slice_in_dim(summed, lax.axis_index("code") * own_rows, own_rows, 0)
    embedded = owned.astype(jnp.bfloat16)
    embed_pad = extend(embedded)
    pre_one = taps_forward(embed_pad, kernel_one)
    hidden = jax.nn.silu(pre_one).astype(jnp.bfloat16)
    hidden_pad = extend(hidden)
    decoded = taps_forward(hidden_pad, kernel_two).astype(jnp.bfloat16)
    grad_hidden = taps_back(extend(upstream), kernel_two)
    sigma = jax.nn.sigmoid(pre_one)
    grad_pre = (grad_hidden * sigma * (1.0 + pre_one * (1.0 - sigma))).astype(jnp.bfloat16)
    grad_embedded = taps_back(extend(grad_pre), kernel_one).astype(jnp.bfloat16)
    piece = lax.all_gather(grad_embedded, "code", axis=0, tiled=True)
    code_terms = lax.dot_general(
        weights.reshape(-1, code_slice),
        piece.reshape(-1, piece.shape[2]),
        (((0,), (0,)), ((), ())),
        preferred_element_type=jnp.float32,
    )
    grad_codebook = lax.psum(code_terms.astype(jnp.bfloat16), ("space", "clip")).astype(jnp.float32)
    term_two = kernel_grad(hidden_pad, upstream)
    term_one = kernel_grad(embed_pad, grad_pre)
    grad_one, grad_two = (
        lax.psum_scatter(term_one, ("space", "code", "clip"), scatter_dimension=3, tiled=True),
        lax.psum_scatter(term_two, ("space", "code", "clip"), scatter_dimension=3, tiled=True),
    )
    return (decoded[None], grad_one, grad_two, grad_codebook)


def solution(mesh):
    in_specs = (
        P("clip", "space", None, "code"),
        P("code", None),
        P(),
        P(),
        P("clip", ("space", "code"), None, None),
    )
    out_specs = (
        P("clip", ("space", "code"), None, None),
        P(None, None, None, ("space", "code", "clip")),
        P(None, None, None, ("space", "code", "clip")),
        P("code", None),
    )
    return jax.shard_map(
        on_device, mesh=mesh, in_specs=in_specs, out_specs=out_specs, check_vma=False
    )
```

profile of v0, /device:TPU:1, one launch (start us, length us, event | category | flops | bytes accessed | tf_op | source)
XLA Modules:
  0.0 509.3 jit_solution(13997313864569233537)
XLA Ops:
  7.2 1.2 copy-done
  8.4 5.7 %fusion = f32[64,32,256]{2,1,0:T(8,128)S(1)} fusion(bf16[1,64,32,2048]{3,2,1,0:T(8,128)(2,1)} %param.5, bf16[2048,256]{1,0:T(8,128)(2,1)S(1)} %copy-done), kind=kOutput, calls=%fused_computation.1 | convolution fusion | flops 2147483648 | bytes 11534336 | tf_op jit(solution)/shard_map/dot_general | solution.py:81
  14.1 44.1 %all-reduce.14 = bf16[64,32,256]{2,1,0:T(8,128)(2,1)} all-reduce(f32[64,32,256]{2,1,0:T(8,128)S(1)} %fusion), channel_id=1, replica_groups=mesh['space'=16,'code'=4,'clip'=2] {'code'}, use_global_device_ids=true, to_apply=%region_0.0 | all-reduce | flops 524288 | bytes 3145728 | tf_op jit(solution)/shard_map/psum | solution.py:85
  58.3 1.1 dynamic-slice_convert_fusion
  59.4 1.9 collective-permute-start
  61.3 5.2 %collective-permute-start.1 = (bf16[1,32,256]{2,1,0:T(8,128)(2,1)S(1)}, bf16[1,32,256]{2,1,0:T(8,128)(2,1)S(1)}, u32[]{:S(2)}, u32[]{:S(2)}) collective-permute-start(bf16[1,32,256]{2,1,0:T(8,128)(2,1)S(1)} %get-tuple-element.55), channel_id=1, source_target_pairs={{2,0},{4,2},{6,4},{8,6},{10,8},{12,10},{14,12},{16,14},{18,16},{20... | collective-permute-start | bytes 49160 | tf_op jit(solution)/shard_map/ppermute | solution.py:15
  66.5 1.9 collective-permute-start.4
  68.5 4.9 collective-permute-start.5
  76.5 1.5 convolution_bitcast_fusion.4
  78.3 0.5 fusion.113
  78.8 0.6 slice-done
  84.6 0.7 fusion.115
  87.6 0.6 fusion.116
  88.3 1.9 collective-permute-start.2
  90.2 4.9 collective-permute-start.3
  95.0 1.9 collective-permute-start.6
  97.0 5.0 collective-permute-start.7
  103.2 2.7 pad_maximum_fusion.1
  105.8 7.3 %copy.12 = f32[3,3,256,512]{2,1,0,3:T(4,128)} copy(f32[3,3,256,512]{3,2,1,0:T(8,128)} %pad_maximum_fusion.1) | data formatting | bytes 9437184 | tf_op jit(solution)/shard_map/stack | solution.py:72
  113.4 2.0 fusion.114
  118.1 0.6 convolution_add_fusion.24
  119.7 1.1 fusion.9
  121.4 1.4 convolution_bitcast_fusion.1
  123.4 1.4 convolution_bitcast_fusion.2
  126.3 1.4 convolution_bitcast_fusion
  127.8 3.4 maximum_bitcast_fusion
  131.2 27.6 %all-gather.2.cloned.1.call-done = bf16[64,32,256]{2,1,0:T(8,128)(2,1)} async-done(((bf16[16,32,256]{2,1,0:T(8,128)(2,1)}), bf16[64,32,256]{2,1,0:T(8,128)(2,1)}) %all-gather.2.cloned.1.call-update) | async-done | bytes 1048592 | tf_op jit(solution)/shard_map/all_gather | solution.py:97
  158.8 7.0 %fusion.2 = bf16[2048,256]{0,1:T(8,128)(2,1)} fusion(bf16[2048,256]{1,0:T(8,128)(2,1)} %bitcast.297, bf16[2048,2048]{1,0:T(8,128)(2,1)} %bitcast.275), kind=kOutput, calls=%fused_computation.8 | convolution fusion | flops 2148007936 | bytes 10485760 | tf_op jit(solution)/shard_map/dot_general | solution.py:98
  166.1 2.3 maximum_bitcast_fusion.2
  168.9 1.0 copy-done.4
  169.9 4.7 pad_maximum_fusion
  174.6 13.8 %copy.13 = f32[3,3,512,512]{2,1,0,3:T(4,128)} copy(f32[3,3,512,512]{3,2,1,0:T(8,128)} %pad_maximum_fusion) | data formatting | bytes 18874368 | tf_op jit(solution)/shard_map/stack | solution.py:72
  188.5 1.7 fusion.32
  190.2 1.5 fusion.14
  191.7 1.5 convolution_add_fusion.13
  193.2 1.5 convolution_add_fusion.12
  194.7 1.6 convolution_add_fusion.11
  196.3 1.5 convolution_add_fusion.10
  197.8 1.5 convolution_add_fusion.9
  199.3 1.5 convolution_add_fusion.8
  200.8 2.4 fusion.7
  203.2 70.1 %all-reduce.11.cloned.1.call-done = bf16[2048,256]{0,1:T(8,128)(2,1)} async-done(((bf16[2048,256]{0,1:T(8,128)(2,1)}), bf16[2048,256]{0,1:T(8,128)(2,1)}) %all-reduce.11.cloned.1.call-update) | async-done | bytes 1048592 | tf_op jit(solution)/shard_map/psum | solution.py:104
  273.2 2.6 copy.16
  275.8 223.9 %all-reduce.13.cloned.1.call-done = (f32[3,3,256,512]{2,1,0,3:T(4,128)}, f32[3,3,512,512]{2,1,0,3:T(4,128)}) async-done(((f32[3,3,256,512]{2,1,0,3:T(4,128)}, f32[3,3,512,512]{2,1,0,3:T(4,128)}), (f32[3,3,256,512]{2,1,0,3:T(4,128)}, f32[3,3,512,512]{2,1,0,3:T(4,128)})) %all-reduce.13.cloned.1.call-update) | async-done | bytes 14155792
  499.7 0.8 constant_dynamic-slice_fusion.1
  500.5 0.9 constant_dynamic-slice_fusion
  501.5 0.7 copy.15
  502.1 0.6 copy.14
  (120 shorter events, 19.2 us)
Async XLA Ops:
  7.2 1.2 copy-start
  7.2 151.6 %all-gather.2.cloned.1.call-start = ((), (), s32[]{:S(2)}) async-start(), calls=%async_computation | async-start | bytes 1310720 | tf_op jit(solution)/shard_map/all_gather | solution.py:97
  14.1 52.4 %copy-start.2 = (bf16[1,16,32,512]{3,2,1,0:T(8,128)(2,1)S(1)}, bf16[1,16,32,512]{3,2,1,0:T(8,128)(2,1)}, u32[]{:S(2)}) copy-start(bf16[1,16,32,512]{3,2,1,0:T(8,128)(2,1)} %param.9) | copy-start | bytes 1572868
  58.3 15.5 %copy-start.5 = (bf16[3,3,256,512]{3,2,1,0:T(8,128)(2,1)S(1)}, bf16[3,3,256,512]{3,2,1,0:T(8,128)(2,1)}, u32[]{:S(2)}) copy-start(bf16[3,3,256,512]{3,2,1,0:T(8,128)(2,1)} %param.7) | copy-start | bytes 7077892
  59.4 13.9 %collective-permute-start = (bf16[1,32,256]{2,1,0:T(8,128)(2,1)S(1)}, bf16[1,32,256]{2,1,0:T(8,128)(2,1)S(1)}, u32[]{:S(2)}, u32[]{:S(2)}) collective-permute-start(bf16[1,32,256]{2,1,0:T(8,128)(2,1)S(1)} %get-tuple-element.54), channel_id=1, source_target_pairs={{0,2},{2,4},{4,6},{6,8},{8,10},{10,12},{12,14},{14,16},{16,18},{18... | collective-permute-start | bytes 49160 | tf_op jit(solution)/shard_map/ppermute | solution.py:12
  61.3 12.0 %collective-permute-start.1 = (bf16[1,32,256]{2,1,0:T(8,128)(2,1)S(1)}, bf16[1,32,256]{2,1,0:T(8,128)(2,1)S(1)}, u32[]{:S(2)}, u32[]{:S(2)}) collective-permute-start(bf16[1,32,256]{2,1,0:T(8,128)(2,1)S(1)} %get-tuple-element.55), channel_id=1, source_target_pairs={{2,0},{4,2},{6,4},{8,6},{10,8},{12,10},{14,12},{16,14},{18,16},{20... | collective-permute-start | bytes 49160 | tf_op jit(solution)/shard_map/ppermute | solution.py:15
  66.5 11.5 %collective-permute-start.4 = (bf16[1,32,512]{2,1,0:T(8,128)(2,1)S(1)}, bf16[1,32,512]{2,1,0:T(8,128)(2,1)S(1)}, u32[]{:S(2)}, u32[]{:S(2)}) collective-permute-start(bf16[1,32,512]{2,1,0:T(8,128)(2,1)S(1)} %get-tuple-element.40), channel_id=1, source_target_pairs={{0,2},{2,4},{4,6},{6,8},{8,10},{10,12},{12,14},{14,16},{16,18},{18... | collective-permute-start | bytes 98312 | tf_op jit(solution)/shard_map/ppermute | solution.py:12
  68.5 9.6 %collective-permute-start.5 = (bf16[1,32,512]{2,1,0:T(8,128)(2,1)S(1)}, bf16[1,32,512]{2,1,0:T(8,128)(2,1)S(1)}, u32[]{:S(2)}, u32[]{:S(2)}) collective-permute-start(bf16[1,32,512]{2,1,0:T(8,128)(2,1)S(1)} %get-tuple-element.41), channel_id=1, source_target_pairs={{2,0},{4,2},{6,4},{8,6},{10,8},{12,10},{14,12},{16,14},{18,16},{20... | collective-permute-start | bytes 98312 | tf_op jit(solution)/shard_map/ppermute | solution.py:15
  76.5 7.6 %copy-start.19 = (f32[512,512]{1,0:T(8,128)}, f32[512,512]{1,0:T(8,128)S(1)}, u32[]{:S(2)}) copy-start(f32[512,512]{1,0:T(8,128)S(1)} %fusion.6) | copy-start | bytes 3145732
  76.5 2.9 slice-start
  78.0 1.7 slice-start.1
  84.1 1.6 copy-start.22
  84.6 3.0 copy-start.6
  84.6 17.8 %copy-start.8 = (bf16[16,32,512]{2,1,0:T(8,128)(2,1)}, bf16[16,32,512]{2,1,0:T(8,128)(2,1)S(1)}, u32[]{:S(2)}) copy-start(bf16[16,32,512]{2,1,0:T(8,128)(2,1)S(1)} %get-tuple-element.14) | copy-start | bytes 1572868
  88.3 24.8 %collective-permute-start.2 = (bf16[1,32,512]{2,1,0:T(8,128)(2,1)}, bf16[1,32,512]{2,1,0:T(8,128)(2,1)S(1)}, u32[]{:S(2)}, u32[]{:S(2)}) collective-permute-start(bf16[1,32,512]{2,1,0:T(8,128)(2,1)} %get-tuple-element.44), channel_id=1, source_target_pairs={{0,2},{2,4},{4,6},{6,8},{8,10},{10,12},{12,14},{14,16},{16,18},{18... | collective-permute-start | bytes 98312 | tf_op jit(solution)/shard_map/ppermute | solution.py:12
  90.2 22.9 %collective-permute-start.3 = (bf16[1,32,512]{2,1,0:T(8,128)(2,1)}, bf16[1,32,512]{2,1,0:T(8,128)(2,1)S(1)}, u32[]{:S(2)}, u32[]{:S(2)}) collective-permute-start(bf16[1,32,512]{2,1,0:T(8,128)(2,1)} %get-tuple-element.45), channel_id=1, source_target_pairs={{2,0},{4,2},{6,4},{8,6},{10,8},{12,10},{14,12},{16,14},{18,16},{20... | collective-permute-start | bytes 98312 | tf_op jit(solution)/shard_map/ppermute | solution.py:15
  95.0 20.3 %collective-permute-start.6 = (bf16[1,32,512]{2,1,0:T(8,128)(2,1)}, bf16[1,32,512]{2,1,0:T(8,128)(2,1)S(1)}, u32[]{:S(2)}, u32[]{:S(2)}) collective-permute-start(bf16[1,32,512]{2,1,0:T(8,128)(2,1)} %get-tuple-element.36), channel_id=1, source_target_pairs={{0,2},{2,4},{4,6},{6,8},{8,10},{10,12},{12,14},{14,16},{16,18},{18... | collective-permute-start | bytes 98312 | tf_op jit(solution)/shard_map/ppermute | solution.py:12
  97.0 18.4 %collective-permute-start.7 = (bf16[1,32,512]{2,1,0:T(8,128)(2,1)}, bf16[1,32,512]{2,1,0:T(8,128)(2,1)S(1)}, u32[]{:S(2)}, u32[]{:S(2)}) collective-permute-start(bf16[1,32,512]{2,1,0:T(8,128)(2,1)} %get-tuple-element.37), channel_id=1, source_target_pairs={{2,0},{4,2},{6,4},{8,6},{10,8},{12,10},{14,12},{16,14},{18,16},{20... | collective-permute-start | bytes 98312 | tf_op jit(solution)/shard_map/ppermute | solution.py:15
  105.8 7.3 %copy-start.7 = (bf16[16,32,512]{2,1,0:T(8,128)(2,1)S(1)}, bf16[16,32,512]{2,1,0:T(8,128)(2,1)}, u32[]{:S(2)}) copy-start(bf16[16,32,512]{2,1,0:T(8,128)(2,1)} %copy-done.6) | copy-start | bytes 1572868
  113.4 2.0 copy-start.9
  116.6 1.2 copy-start.20
  116.6 1.5 copy-start.23
  120.8 152.5 %all-reduce.11.cloned.1.call-start = ((), (), s32[]{:S(2)}) async-start(), calls=%async_computation.1 | async-start | bytes 2097152 | tf_op jit(solution)/shard_map/psum | solution.py:104
  120.9 2.4 copy-start.17
  120.9 1.9 copy-start.11
  121.4 1.9 copy-start.10
  122.9 1.9 copy-start.12
  123.3 1.9 copy-start.13
  124.8 1.0 copy-start.16
  125.3 1.1 copy-start.14
  125.7 2.0 copy-start.24
  165.8 333.9 %all-reduce.13.cloned.1.call-start = ((), (), s32[]{:S(2)}) async-start(), calls=%async_computation.2 | async-start | bytes 37748736
  166.1 2.8 copy-start.3
  166.1 3.8 copy-start.4
  188.5 1.7 copy-start.15
  188.5 3.2 copy-start.18
  194.7 1.6 copy-start.21
  200.8 302.0 %copy-start.1 = (bf16[2048,256]{1,0:T(8,128)(2,1)S(1)}, bf16[2048,256]{1,0:T(8,128)(2,1)}, u32[]{:S(2)}) copy-start(bf16[2048,256]{1,0:T(8,128)(2,1)} %param.6) | copy-start | bytes 3145732
Sparse Core Ops, SparseCore 0:
  120.9 37.8 all-gather.1
  166.0 107.2 all-reduce.10
  278.8 220.8 all-reduce.12
where the time goes:
time: 511 us; the launch traced here: 509 us
  waiting for transfers between devices  322 us (63%)
  matrix products  49.1 us (10%)
  blocking collectives  44.1 us (9%)
  local copies, waits for them, and re-layouts  36.6 us (7%)
  starting transfers between devices  27.9 us (5%)
  other arithmetic  15.2 us (3%)
  between operations  14.6 us (3%)
    unnamed x4, waiting for transfers between devices  224 us
    psum x1, waiting for transfers between devices, on_device(): lax.psum(code_terms.astype(jnp.bfloat16), ('space', 'clip'))  70.1 us
    psum x1, blocking collectives, on_device(): summed = lax.psum(partial_value, 'code')  44.1 us
    all_gather x1, waiting for transfers between devices, on_device(): piece = lax.all_gather(grad_embedded, 'code', axis=0, tiled=True)  27.6 us
    another operation x2, local copies, waits for them, and re-layouts, kernel_grad(): return jnp.stack(result)  21.1 us
    ppermute x4, starting transfers between devices, with_halo(): lax.ppermute(lax.slice_in_dim(block, 0, width, axis=dim), axis, backward)  19.9 us
    dot_general x18, matrix products, taps_forward(): jnp.dot(window, kernel[first, second], preferred_element_type=jnp.float32)  17.2 us
    another operation x6, other arithmetic, kernel_grad(): return jnp.stack(result)  13.6 us
  transfers between devices with their start and end apart: 11, of which 3 were waited for; matrix products, arithmetic and copies ran while one was open for 13% of the time, Pallas kernels for 0%

commit v1 on v0

--- a/solution.py
+++ b/solution.py
@@ -94,7 +94,10 @@
     sigma = jax.nn.sigmoid(pre_one)
     grad_pre = (grad_hidden * sigma * (1.0 + pre_one * (1.0 - sigma))).astype(jnp.bfloat16)
     grad_embedded = taps_back(extend(grad_pre), kernel_one).astype(jnp.bfloat16)
-    piece = lax.all_gather(grad_embedded, "code", axis=0, tiled=True)
+    outcome_arr = lax.psum(1, "code")
+    t1 = jnp.stack([grad_embedded] * outcome_arr)
+    seen_now = lax.all_to_all(t1, "code", 0, 0)
+    piece = jnp.concatenate(seen_now, axis=0)
     code_terms = lax.dot_general(
         weights.reshape(-1, code_slice),
         piece.reshape(-1, piece.shape[2]),

time: 511 us -> 510 us (level)
  waiting for transfers between devices: 322 us -> 310 us
  starting transfers between devices: 27.9 us -> 34.3 us
    all_gather x1 -> x0, waiting for transfers between devices: 27.6 us -> none  [on_device(): piece = lax.all_gather(grad_embedded, 'code', axis=0, tiled=True)]
    psum x1, waiting for transfers between devices: 70.1 us -> 80.9 us  [on_device(): lax.psum(code_terms.astype(jnp.bfloat16), ('space', 'clip'))]
    all_to_all x0 -> x1, starting transfers between devices: none -> 6.43 us  [on_device(): seen_now = lax.all_to_all(t1, 'code', 0, 0)]
    unnamed x59 -> x73, local copies, waits for them, and re-layouts: 9.85 us -> 11.2 us
    unnamed x4 -> x3, waiting for transfers between devices: 224 us -> 224 us
where the time goes in v1:
time: 510 us; the launch traced here: 508 us
  waiting for transfers between devices  310 us (61%)
  matrix products  51.2 us (10%)
  blocking collectives  44.1 us (9%)
  local copies, waits for them, and re-layouts  38.5 us (8%)
  starting transfers between devices  34.3 us (7%)
  other arithmetic  15.2 us (3%)
  between operations  14.9 us (3%)
    unnamed x3, waiting for transfers between devices  224 us
    psum x1, waiting for transfers between devices, on_device(): lax.psum(code_terms.astype(jnp.bfloat16), ('space', 'clip'))  80.9 us
    psum x1, blocking collectives, on_device(): summed = lax.psum(partial_value, 'code')  44.1 us
    another operation x2, local copies, waits for them, and re-layouts, kernel_grad(): return jnp.stack(result)  21.1 us
    ppermute x4, starting transfers between devices, with_halo(): lax.ppermute(lax.slice_in_dim(block, 0, width, axis=dim), axis, backward)  19.9 us
    dot_general x18, matrix products, taps_forward(): jnp.dot(window, kernel[first, second], preferred_element_type=jnp.float32)  17.2 us
    dot_general x18, matrix products, kernel_grad(): lax.dot_general(window, flat_up, (((0,), (0,)), ((), ())), preferred_elem...  14 us
    another operation x6, other arithmetic, kernel_grad(): return jnp.stack(result)  13.6 us
  transfers between devices with their start and end apart: 11, of which 3 were waited for; matrix products, arithmetic and copies ran while one was open for 13% of the time, Pallas kernels for 0%

profile of v1, /device:TPU:1, one launch (start us, length us, event | category | flops | bytes accessed | tf_op | source)
XLA Modules:
  0.0 508.1 jit_solution(2508180612318628669)
XLA Ops:
  7.2 1.2 copy-done
  8.4 5.7 %fusion = f32[64,32,256]{2,1,0:T(8,128)S(1)} fusion(bf16[1,64,32,2048]{3,2,1,0:T(8,128)(2,1)} %param.5, bf16[2048,256]{1,0:T(8,128)(2,1)S(1)} %copy-done), kind=kOutput, calls=%fused_computation.1 | convolution fusion | flops 2147483648 | bytes 11534336 | tf_op jit(solution)/shard_map/dot_general | solution.py:81
  14.1 44.1 %all-reduce.14 = bf16[64,32,256]{2,1,0:T(8,128)(2,1)} all-reduce(f32[64,32,256]{2,1,0:T(8,128)S(1)} %fusion), channel_id=1, replica_groups=mesh['space'=16,'code'=4,'clip'=2] {'code'}, use_global_device_ids=true, to_apply=%region_0.0 | all-reduce | flops 524288 | bytes 3145728 | tf_op jit(solution)/shard_map/psum | solution.py:85
  58.3 1.1 dynamic-slice_convert_fusion
  59.4 1.9 collective-permute-start
  61.3 5.2 %collective-permute-start.1 = (bf16[1,32,256]{2,1,0:T(8,128)(2,1)S(1)}, bf16[1,32,256]{2,1,0:T(8,128)(2,1)S(1)}, u32[]{:S(2)}, u32[]{:S(2)}) collective-permute-start(bf16[1,32,256]{2,1,0:T(8,128)(2,1)S(1)} %get-tuple-element.55), channel_id=1, source_target_pairs={{2,0},{4,2},{6,4},{8,6},{10,8},{12,10},{14,12},{16,14},{18,16},{20... | collective-permute-start | bytes 49160 | tf_op jit(solution)/shard_map/ppermute | solution.py:15
  66.5 1.9 collective-permute-start.4
  68.5 4.9 collective-permute-start.5
  76.5 1.5 convolution_bitcast_fusion.4
  84.6 0.7 fusion.115
  88.3 1.9 collective-permute-start.2
  90.2 4.9 collective-permute-start.3
  95.1 1.9 collective-permute-start.6
  97.0 5.0 collective-permute-start.7
  103.2 2.7 pad_maximum_fusion.1
  105.9 7.3 %copy.12 = f32[3,3,256,512]{2,1,0,3:T(4,128)} copy(f32[3,3,256,512]{3,2,1,0:T(8,128)} %pad_maximum_fusion.1) | data formatting | bytes 9437184 | tf_op jit(solution)/shard_map/stack | solution.py:72
  113.3 1.5 convolution_bitcast_fusion.7
  114.7 1.4 convolution_bitcast_fusion.1
  116.4 1.4 fusion.114
  117.8 0.8 copy-done.16
  118.7 1.4 convolution_bitcast_fusion.3
  120.1 1.4 convolution_bitcast_fusion.2
  121.5 1.4 convolution_bitcast_fusion.5
  127.7 1.1 stack.135
  128.8 6.4 %all-to-all-start = ((bf16[4,16,32,256]{3,2,1,0:T(8,128)(2,1)}), bf16[4,16,32,256]{3,2,1,0:T(8,128)(2,1)S(1)}, u32[]{:S(2)}, u32[]{:S(2)}) async-start(bf16[4,16,32,256]{3,2,1,0:T(8,128)(2,1)} %stack.135), calls=%async_computation | async-start | bytes 2097152 | tf_op jit(solution)/shard_map/all_to_all | solution.py:99
  136.3 1.5 convolution_bitcast_fusion
  138.3 3.4 maximum_bitcast_fusion
  141.7 4.8 all-to-all-done
  146.5 6.7 %fusion.2 = bf16[2048,256]{0,1:T(8,128)(2,1)} fusion(bf16[2048,256]{1,0:T(8,128)(2,1)S(1)} %bitcast.278, bf16[2048,2048]{1,0:T(8,128)(2,1)} %bitcast.275), kind=kOutput, calls=%fused_computation.8 | convolution fusion | flops 2148007936 | bytes 10485760 | tf_op jit(solution)/shard_map/dot_general | solution.py:101
  153.5 2.3 maximum_bitcast_fusion.2
  156.3 1.0 copy-done.4
  157.3 4.7 pad_maximum_fusion
  162.0 13.8 %copy.13 = f32[3,3,512,512]{2,1,0,3:T(4,128)} copy(f32[3,3,512,512]{3,2,1,0:T(8,128)} %pad_maximum_fusion) | data formatting | bytes 18874368 | tf_op jit(solution)/shard_map/stack | solution.py:72
  175.8 1.5 fusion.32
  177.4 1.5 fusion.14
  178.9 1.5 convolution_add_fusion.13
  180.4 1.5 convolution_add_fusion.12
  181.9 1.6 convolution_add_fusion.11
  183.5 1.6 convolution_add_fusion.10
  185.1 1.5 convolution_add_fusion.9
  186.7 1.5 convolution_add_fusion.8
  188.2 2.4 fusion.7
  190.6 80.9 %all-reduce.11.cloned.1.call-done = bf16[2048,256]{0,1:T(8,128)(2,1)} async-done(((bf16[2048,256]{0,1:T(8,128)(2,1)}), bf16[2048,256]{0,1:T(8,128)(2,1)}) %all-reduce.11.cloned.1.call-update) | async-done | bytes 1048592 | tf_op jit(solution)/shard_map/psum | solution.py:107
  271.6 2.6 copy.16
  274.1 224.1 %all-reduce.13.cloned.1.call-done = (f32[3,3,256,512]{2,1,0,3:T(4,128)}, f32[3,3,512,512]{2,1,0,3:T(4,128)}) async-done(((f32[3,3,256,512]{2,1,0,3:T(4,128)}, f32[3,3,512,512]{2,1,0,3:T(4,128)}), (f32[3,3,256,512]{2,1,0,3:T(4,128)}, f32[3,3,512,512]{2,1,0,3:T(4,128)})) %all-reduce.13.cloned.1.call-update) | async-done | bytes 14155792
  498.3 0.8 constant_dynamic-slice_fusion.1
  499.1 0.9 constant_dynamic-slice_fusion
  500.0 0.7 copy.15
  (134 shorter events, 21.5 us)
Async XLA Ops:
  7.2 1.2 copy-start
  14.1 52.4 %copy-start.2 = (bf16[1,16,32,512]{3,2,1,0:T(8,128)(2,1)S(1)}, bf16[1,16,32,512]{3,2,1,0:T(8,128)(2,1)}, u32[]{:S(2)}) copy-start(bf16[1,16,32,512]{3,2,1,0:T(8,128)(2,1)} %param.9) | copy-start | bytes 1572868
  58.3 15.5 %copy-start.5 = (bf16[3,3,256,512]{3,2,1,0:T(8,128)(2,1)S(1)}, bf16[3,3,256,512]{3,2,1,0:T(8,128)(2,1)}, u32[]{:S(2)}) copy-start(bf16[3,3,256,512]{3,2,1,0:T(8,128)(2,1)} %param.7) | copy-start | bytes 7077892
  59.4 13.9 %collective-permute-start = (bf16[1,32,256]{2,1,0:T(8,128)(2,1)S(1)}, bf16[1,32,256]{2,1,0:T(8,128)(2,1)S(1)}, u32[]{:S(2)}, u32[]{:S(2)}) collective-permute-start(bf16[1,32,256]{2,1,0:T(8,128)(2,1)S(1)} %get-tuple-element.54), channel_id=1, source_target_pairs={{0,2},{2,4},{4,6},{6,8},{8,10},{10,12},{12,14},{14,16},{16,18},{18... | collective-permute-start | bytes 49160 | tf_op jit(solution)/shard_map/ppermute | solution.py:12
  61.3 12.0 %collective-permute-start.1 = (bf16[1,32,256]{2,1,0:T(8,128)(2,1)S(1)}, bf16[1,32,256]{2,1,0:T(8,128)(2,1)S(1)}, u32[]{:S(2)}, u32[]{:S(2)}) collective-permute-start(bf16[1,32,256]{2,1,0:T(8,128)(2,1)S(1)} %get-tuple-element.55), channel_id=1, source_target_pairs={{2,0},{4,2},{6,4},{8,6},{10,8},{12,10},{14,12},{16,14},{18,16},{20... | collective-permute-start | bytes 49160 | tf_op jit(solution)/shard_map/ppermute | solution.py:15
  66.5 11.5 %collective-permute-start.4 = (bf16[1,32,512]{2,1,0:T(8,128)(2,1)S(1)}, bf16[1,32,512]{2,1,0:T(8,128)(2,1)S(1)}, u32[]{:S(2)}, u32[]{:S(2)}) collective-permute-start(bf16[1,32,512]{2,1,0:T(8,128)(2,1)S(1)} %get-tuple-element.40), channel_id=1, source_target_pairs={{0,2},{2,4},{4,6},{6,8},{8,10},{10,12},{12,14},{14,16},{16,18},{18... | collective-permute-start | bytes 98312 | tf_op jit(solution)/shard_map/ppermute | solution.py:12
  68.5 9.5 %collective-permute-start.5 = (bf16[1,32,512]{2,1,0:T(8,128)(2,1)S(1)}, bf16[1,32,512]{2,1,0:T(8,128)(2,1)S(1)}, u32[]{:S(2)}, u32[]{:S(2)}) collective-permute-start(bf16[1,32,512]{2,1,0:T(8,128)(2,1)S(1)} %get-tuple-element.41), channel_id=1, source_target_pairs={{2,0},{4,2},{6,4},{8,6},{10,8},{12,10},{14,12},{16,14},{18,16},{20... | collective-permute-start | bytes 98312 | tf_op jit(solution)/shard_map/ppermute | solution.py:15
  76.5 7.6 %copy-start.23 = (f32[512,512]{1,0:T(8,128)}, f32[512,512]{1,0:T(8,128)S(1)}, u32[]{:S(2)}) copy-start(f32[512,512]{1,0:T(8,128)S(1)} %fusion.6) | copy-start | bytes 3145732
  76.5 2.9 slice-start
  78.0 1.7 slice-start.1
  84.1 1.6 copy-start.29
  84.6 3.0 copy-start.8
  84.6 17.9 %copy-start.6 = (bf16[16,32,512]{2,1,0:T(8,128)(2,1)}, bf16[16,32,512]{2,1,0:T(8,128)(2,1)S(1)}, u32[]{:S(2)}) copy-start(bf16[16,32,512]{2,1,0:T(8,128)(2,1)S(1)} %get-tuple-element.14) | copy-start | bytes 1572868
  88.3 24.8 %collective-permute-start.2 = (bf16[1,32,512]{2,1,0:T(8,128)(2,1)}, bf16[1,32,512]{2,1,0:T(8,128)(2,1)S(1)}, u32[]{:S(2)}, u32[]{:S(2)}) collective-permute-start(bf16[1,32,512]{2,1,0:T(8,128)(2,1)} %get-tuple-element.44), channel_id=1, source_target_pairs={{0,2},{2,4},{4,6},{6,8},{8,10},{10,12},{12,14},{14,16},{16,18},{18... | collective-permute-start | bytes 98312 | tf_op jit(solution)/shard_map/ppermute | solution.py:12
  90.2 22.9 %collective-permute-start.3 = (bf16[1,32,512]{2,1,0:T(8,128)(2,1)}, bf16[1,32,512]{2,1,0:T(8,128)(2,1)S(1)}, u32[]{:S(2)}, u32[]{:S(2)}) collective-permute-start(bf16[1,32,512]{2,1,0:T(8,128)(2,1)} %get-tuple-element.45), channel_id=1, source_target_pairs={{2,0},{4,2},{6,4},{8,6},{10,8},{12,10},{14,12},{16,14},{18,16},{20... | collective-permute-start | bytes 98312 | tf_op jit(solution)/shard_map/ppermute | solution.py:15
  95.1 27.9 %collective-permute-start.6 = (bf16[1,32,512]{2,1,0:T(8,128)(2,1)}, bf16[1,32,512]{2,1,0:T(8,128)(2,1)S(1)}, u32[]{:S(2)}, u32[]{:S(2)}) collective-permute-start(bf16[1,32,512]{2,1,0:T(8,128)(2,1)} %get-tuple-element.36), channel_id=1, source_target_pairs={{0,2},{2,4},{4,6},{6,8},{8,10},{10,12},{12,14},{14,16},{16,18},{18... | collective-permute-start | bytes 98312 | tf_op jit(solution)/shard_map/ppermute | solution.py:12
  97.0 26.0 %collective-permute-start.7 = (bf16[1,32,512]{2,1,0:T(8,128)(2,1)}, bf16[1,32,512]{2,1,0:T(8,128)(2,1)S(1)}, u32[]{:S(2)}, u32[]{:S(2)}) collective-permute-start(bf16[1,32,512]{2,1,0:T(8,128)(2,1)} %get-tuple-element.37), channel_id=1, source_target_pairs={{2,0},{4,2},{6,4},{8,6},{10,8},{12,10},{14,12},{16,14},{18,16},{20... | collective-permute-start | bytes 98312 | tf_op jit(solution)/shard_map/ppermute | solution.py:15
  105.9 7.3 %copy-start.9 = (bf16[16,32,512]{2,1,0:T(8,128)(2,1)S(1)}, bf16[16,32,512]{2,1,0:T(8,128)(2,1)}, u32[]{:S(2)}) copy-start(bf16[16,32,512]{2,1,0:T(8,128)(2,1)} %copy-done.8) | copy-start | bytes 1572868
  113.2 1.5 copy-start.10
  113.2 2.9 copy-start.12
  117.8 0.8 copy-start.16
  117.8 5.1 %copy-start.14 = (bf16[16,32,512]{2,1,0:T(8,128)(2,1)}, bf16[16,32,512]{2,1,0:T(8,128)(2,1)S(1)}, u32[]{:S(2)}) copy-start(bf16[16,32,512]{2,1,0:T(8,128)(2,1)S(1)} %get-tuple-element.28) | copy-start | bytes 1572868
  117.8 5.2 %copy-start.18 = (bf16[16,32,512]{2,1,0:T(8,128)(2,1)}, bf16[16,32,512]{2,1,0:T(8,128)(2,1)S(1)}, u32[]{:S(2)}) copy-start(bf16[16,32,512]{2,1,0:T(8,128)(2,1)S(1)} %get-tuple-element.30) | copy-start | bytes 1572868
  120.1 2.9 copy-start.7
  124.2 1.2 copy-start.24
  124.2 1.5 copy-start.30
  127.4 7.9 %copy-start.20 = (bf16[16,32,512]{2,1,0:T(8,128)(2,1)S(1)}, bf16[16,32,512]{2,1,0:T(8,128)(2,1)}, u32[]{:S(2)}) copy-start(bf16[16,32,512]{2,1,0:T(8,128)(2,1)} %get-tuple-element.31) | copy-start | bytes 1572868
  128.8 6.9 %copy-start.22 = (bf16[16,32,512]{2,1,0:T(8,128)(2,1)S(1)}, bf16[16,32,512]{2,1,0:T(8,128)(2,1)}, u32[]{:S(2)}) copy-start(bf16[16,32,512]{2,1,0:T(8,128)(2,1)} %get-tuple-element.32) | copy-start | bytes 1572868
  128.8 17.6 %all-to-all-start = ((bf16[4,16,32,256]{3,2,1,0:T(8,128)(2,1)}), bf16[4,16,32,256]{3,2,1,0:T(8,128)(2,1)S(1)}, u32[]{:S(2)}, u32[]{:S(2)}) async-start(bf16[4,16,32,256]{3,2,1,0:T(8,128)(2,1)} %stack.135), calls=%async_computation | async-start | bytes 2097152 | tf_op jit(solution)/shard_map/all_to_all | solution.py:99
  135.3 1.0 copy-start.21
  135.3 136.3 %all-reduce.11.cloned.1.call-start = ((), (), s32[]{:S(2)}) async-start(), calls=%async_computation.1 | async-start | bytes 2097152 | tf_op jit(solution)/shard_map/psum | solution.py:107
  135.7 2.1 copy-start.26
  135.7 2.1 copy-start.27
  135.7 2.1 copy-start.28
  135.8 2.6 copy-start.31
  153.2 345.0 %all-reduce.13.cloned.1.call-start = ((), (), s32[]{:S(2)}) async-start(), calls=%async_computation.2 | async-start | bytes 37748736
  153.5 2.8 copy-start.3
  153.5 3.8 copy-start.4
  175.8 3.0 copy-start.13
  180.4 1.6 copy-start.19
  181.9 1.6 copy-start.25
  183.5 1.6 copy-start.17
  185.1 1.6 copy-start.15
  186.7 1.6 copy-start.11
  188.2 313.0 %copy-start.1 = (bf16[2048,256]{1,0:T(8,128)(2,1)S(1)}, bf16[2048,256]{1,0:T(8,128)(2,1)}, u32[]{:S(2)}) copy-start(bf16[2048,256]{1,0:T(8,128)(2,1)} %param.6) | copy-start | bytes 3145732
Sparse Core Ops, SparseCore 0:
  153.3 118.1 all-reduce.10
  277.1 221.0 all-reduce.12
